TPU v7x, 128 devices: a whole 4x4x4 slice. The times are simulated.
128 devices in a mesh: ctx: 16 (over z, y), head: 8 (over x, core).
Axes of the slice: x: 4, y: 4, z: 4, core: 2. Of those that a mesh axis runs over, the one named last changes fastest.
Arguments:
- query_states: bfloat16 [16384, 128, 128], P(('ctx', 'head')), may hold values from -8 to 8
- key_states: bfloat16 [16384, 8, 128], P(('ctx', 'head')), may hold values from -8 to 8
- value_states: bfloat16 [16384, 8, 128], P(('ctx', 'head')), may hold values from -6 to 6
- slash_offsets: int32 [8, 256, 12], P('head'), may hold values from 0 to 31, as said below
- slash_counts: int32 [8, 256], P('head'), may hold values from 1 to 12, as said below
- vertical_blocks: int32 [8, 256, 12], P('head'), may hold values from 0 to 223, as said below
- vertical_counts: int32 [8, 256], P('head'), may hold values from 0 to 12, as said below
Outputs:
- attended: bfloat16 [16384, 128, 128], P(('ctx', 'head'))
Inputs may be any that keep to these rules, and one draw needn't show every extreme that they name: `slash_offsets`: for every head and query block b, the entries j < slash_counts are distinct, at most b and below 32; entry 0 is 0; the other entries are 0. `slash_counts`: at most min(12, b + 1) for query block b. `vertical_blocks`: for every head and query block b, the entries j < vertical_counts are distinct blocks at most b - 32; the other entries are 0. `vertical_counts`: at most max(0, b - 31) for query block b.
All inputs are finite; a program needn't handle non-finite values.
Results may differ from a plain program's by a relative error of at most 0.0049.
Values may be sent and summed in bfloat16 or wider, within the bound.
A program may use at most 128 MiB of HBM per device.

v0:
```python
import jax
import jax.numpy as jnp
from jax import lax
from jax.sharding import PartitionSpec as P

BLK = 64
G = 16


NEG = -1e30


def visit(carry_state, query_group, key_table, value_table, query_ids, blocks, live_slots):
    maxima, totals, running = carry_state
    group_count, block_len, local_groups, group_heads, head_dim = query_group.shape
    head_lanes = jnp.arange(local_groups, dtype=jnp.int32)[None, :, None]
    key_tiles = key_table[blocks, :, head_lanes].reshape(
        group_count, local_groups, 2 * block_len, head_dim
    )
    value_tiles = value_table[blocks, :, head_lanes].reshape(
        group_count, local_groups, 2 * block_len, head_dim
    )
    scores = jnp.einsum(
        "bqngd,bnsd->bngqs", query_group, key_tiles, preferred_element_type=jnp.float32
    ) * head_dim ** (-0.5)
    within = jnp.arange(block_len, dtype=jnp.int32)
    key_pos = (blocks[..., None] * block_len + within).reshape(
        group_count, local_groups, 2 * block_len
    )
    key_live = jnp.repeat(live_slots, block_len, axis=2)
    query_pos = query_ids[:, None] * block_len + within
    visible = key_live[:, :, None, :] & (key_pos[:, :, None, :] <= query_pos[:, None, :, None])
    visible = visible[:, :, None]
    masked = jnp.where(visible, scores, NEG)
    new_max = jnp.maximum(maxima, jnp.max(masked, axis=-1))
    decay_old = jnp.exp(maxima - new_max)
    probs = jnp.where(visible, jnp.exp(scores - new_max[..., None]), 0.0)
    totals = totals * decay_old + jnp.sum(probs, axis=-1)
    running = running * decay_old[..., None] + jnp.einsum(
        "bngqs,bnsd->bngqd",
        probs.astype(jnp.bfloat16),
        value_tiles,
        preferred_element_type=jnp.float32,
    )
    return (new_max, totals, running)


def attend(
    query_group,
    query_ids,
    key_table,
    value_table,
    slash_offsets,
    slash_counts,
    vertical_blocks,
    vertical_counts,
):
    group_count, block_len, local_groups, group_heads, head_dim = query_group.shape
    slash_list = jnp.transpose(slash_offsets[:, query_ids], (1, 0, 2))
    slash_live = jnp.transpose(slash_counts[:, query_ids])
    vertical_list = jnp.transpose(vertical_blocks[:, query_ids], (1, 0, 2))
    vertical_live = jnp.transpose(vertical_counts[:, query_ids])
    state_shape = (group_count, local_groups, group_heads, block_len)
    carry_state = (
        jnp.full(state_shape, NEG, jnp.float32),
        jnp.zeros(state_shape, jnp.float32),
        jnp.zeros(state_shape + (head_dim,), jnp.float32),
    )
    couple = jnp.arange(2, dtype=jnp.int32)

    def slash_step(turn, state_now):
        picked = lax.dynamic_slice_in_dim(slash_list, 2 * turn, 2, axis=2)
        blocks = query_ids[:, None, None] - picked
        live_slots = (2 * turn + couple)[None, None, :] < slash_live[:, :, None]
        return visit(state_now, query_group, key_table, value_table, query_ids, blocks, live_slots)

    def vertical_step(turn, state_now):
        blocks = lax.dynamic_slice_in_dim(vertical_list, 2 * turn, 2, axis=2)
        live_slots = (2 * turn + couple)[None, None, :] < vertical_live[:, :, None]
        return visit(state_now, query_group, key_table, value_table, query_ids, blocks, live_slots)

    carry_state = lax.fori_loop(0, (jnp.max(slash_live) + 1) // 2, slash_step, carry_state)
    carry_state = lax.fori_loop(0, (jnp.max(vertical_live) + 1) // 2, vertical_step, carry_state)
    maxima, totals, running = carry_state
    result = (running / totals[..., None]).astype(jnp.bfloat16)
    return jnp.transpose(result, (0, 3, 1, 2, 4)).reshape(
        group_count * block_len, local_groups * group_heads, head_dim
    )


def on_device(
    query_states,
    key_states,
    value_states,
    slash_offsets,
    slash_counts,
    vertical_blocks,
    vertical_counts,
):
    ctx_rank = lax.axis_index("ctx")
    query_local, key_local, value_local = (
        lax.all_to_all(query_states, "head", split_axis=1, concat_axis=0, tiled=True),
        lax.all_to_all(key_states, "head", split_axis=1, concat_axis=0, tiled=True),
        lax.all_to_all(value_states, "head", split_axis=1, concat_axis=0, tiled=True),
    )
    key_full, value_full = (
        lax.all_gather(key_local, "ctx", axis=0, tiled=True),
        lax.all_gather(value_local, "ctx", axis=0, tiled=True),
    )
    local_rows, heads_local, head_dim = query_local.shape
    local_groups = heads_local // G
    seq_blocks = key_full.shape[0] // BLK
    key_table = key_full.reshape(seq_blocks, BLK, local_groups, head_dim)
    value_table = value_full.reshape(seq_blocks, BLK, local_groups, head_dim)
    query_blocks = local_rows // BLK
    query_ids = ctx_rank * query_blocks + jnp.arange(query_blocks, dtype=jnp.int32)
    group_size = 512 // BLK
    group_total = query_blocks // group_size
    query_grouped = query_local.reshape(group_total, group_size, BLK, local_groups, G, head_dim)

    def run_group(entries):
        return attend(
            entries[0],
            entries[1],
            key_table,
            value_table,
            slash_offsets,
            slash_counts,
            vertical_blocks,
            vertical_counts,
        )

    answers = lax.map(run_group, (query_grouped, query_ids.reshape(group_total, group_size)))
    answers = answers.reshape(local_rows, heads_local, head_dim)
    return lax.all_to_all(answers, "head", split_axis=0, concat_axis=1, tiled=True)


def solution(mesh):
    in_specs = (
        P(("ctx", "head"), None, None),
        P(("ctx", "head"), None, None),
        P(("ctx", "head"), None, None),
        P("head", None, None),
        P("head", None),
        P("head", None, None),
        P("head", None),
    )
    out_specs = P(("ctx", "head"), None, None)
    return jax.shard_map(
        on_device, mesh=mesh, in_specs=in_specs, out_specs=out_specs, check_vma=False
    )
```

profile of v0, /device:TPU:96, one launch (start us, length us, event | category | flops | bytes accessed | tf_op | source)
XLA Modules:
  0.0 660.0 jit_solution(3249853632355213992)
XLA Ops:
  7.5 11.7 %all_to_all.69 = bf16[128,8,128]{2,0,1:T(8,128)(2,1)} all-to-all(bf16[128,8,128]{2,0,1:T(8,128)(2,1)S(1)} %copy.89), channel_id=1, replica_groups=mesh['ctx'=16,'head'=8] {'head'}, dimensions={1} | all-to-all | bytes 524288 | tf_op jit(solution)/shard_map/all_to_all | solution.py:103
  20.3 10.6 %all_to_all.70 = bf16[128,8,128]{2,0,1:T(8,128)(2,1)} all-to-all(bf16[128,8,128]{2,0,1:T(8,128)(2,1)S(1)} %copy.90), channel_id=1, replica_groups=mesh['ctx'=16,'head'=8] {'head'}, dimensions={1} | all-to-all | bytes 524288 | tf_op jit(solution)/shard_map/all_to_all | solution.py:104
  30.9 6.8 %copy.86 = bf16[128,128,128]{2,0,1:T(8,128)(2,1)} copy(bf16[128,128,128]{2,1,0:T(8,128)(2,1)} %param.13) | data formatting | bytes 8388608 | tf_op args[0]
  42.7 49.4 %all-to-all-done = bf16[128,128,128]{2,0,1:T(8,128)(2,1)} async-done(((bf16[128,128,128]{2,0,1:T(8,128)(2,1)}), bf16[128,128,128]{2,0,1:T(8,128)(2,1)}, u32[]{:S(2)}, u32[]{:S(2)}) %all-to-all-start) | async-done | bytes 4194336 | tf_op jit(solution)/shard_map/all_to_all | solution.py:102
  92.1 6.9 %copy.88 = bf16[8,128,16,128]{3,2,1,0:T(8,128)(2,1)} copy(bf16[8,128,16,128]{3,1,2,0:T(8,128)(2,1)} %bitcast.17) | data formatting | bytes 8388608 | tf_op jit(solution)/shard_map/all_to_all | solution.py:102
  99.0 24.4 %all-gather.5.cloned.1.call-done = bf16[16384,1,128]{2,0,1:T(8,128)(2,1)} async-done(((bf16[1024,1,128]{2,0,1:T(8,128)(2,1)}), bf16[16384,1,128]{2,0,1:T(8,128)(2,1)}) %all-gather.5.cloned.1.call-update) | async-done | bytes 4194320 | tf_op jit(solution)/shard_map/all_gather | solution.py:108
  123.4 472.6 %while.81 = (s32[]{:T(128)}, bf16[2,512,16,128]{3,2,1,0:T(8,128)(2,1)}, s32[2,8]{1,0:T(2,128)S(1)}, s32[1,256]{1,0:T(1,128)S(1)}, s32[1,256,12]{2,1,0:T(8,128)S(...) while((s32[]{:T(128)}, ...), condition=%wide.region_11.12_spmd, body=%wide.region_0.11_spmd.sunk | while | flops 1103417728 | bytes 111853656 | solution.py:133
  130.9 110.1 %while.82 = (s32[]{:T(128)}, f32[8,1,16,64]{3,2,0,1:T(8,128)S(1)}, f32[8,1,16,64]{3,2,0,1:T(8,128)S(1)}, f32[8,1,16,64,128]{4,3,2,0,1:T(8,128)}, s32[]{:T(128)},...) while((s32[]{:T(128)}, f32[8,1,16,64]{3,2,0,1:T(8,128)S(1)}, ...), condition=%wide.region_5.5_spmd.clone, body=%wide.region_2.4_spmd.clone.sunk | while | flops 550659776 | bytes 42241712 | solution.py:82
  140.7 6.1 bitcast_add_fusion.9
  177.4 6.1 bitcast_add_fusion.9
  195.7 6.1 bitcast_add_fusion.9
  232.4 6.1 bitcast_add_fusion.9
  243.6 110.1 %while.83 = (s32[]{:T(128)}, f32[8,1,16,64]{3,2,0,1:T(8,128)S(1)}, f32[8,1,16,64]{3,2,0,1:T(8,128)S(1)}, f32[8,1,16,64,128]{4,3,2,0,1:T(8,128)}, s32[]{:T(128)},...) while((s32[]{:T(128)}, f32[8,1,16,64]{3,2,0,1:T(8,128)S(1)}, ...), condition=%wide.region_10.10_spmd.clone, body=%wide.region_7.9_spmd.clone.sunk | while | flops 550659712 | bytes 42241680 | solution.py:83
  253.4 6.1 bitcast_add_fusion.11
  271.7 6.1 bitcast_add_fusion.11
  290.1 6.1 bitcast_add_fusion.11
  308.4 6.1 bitcast_add_fusion.11
  326.8 6.1 bitcast_add_fusion.11
  345.1 6.1 bitcast_add_fusion.11
  367.2 110.1 %while.82 = (s32[]{:T(128)}, f32[8,1,16,64]{3,2,0,1:T(8,128)S(1)}, f32[8,1,16,64]{3,2,0,1:T(8,128)S(1)}, f32[8,1,16,64,128]{4,3,2,0,1:T(8,128)}, s32[]{:T(128)},...) while((s32[]{:T(128)}, f32[8,1,16,64]{3,2,0,1:T(8,128)S(1)}, ...), condition=%wide.region_5.5_spmd.clone, body=%wide.region_2.4_spmd.clone.sunk | while | flops 550659776 | bytes 42241712 | solution.py:82
  395.3 6.1 bitcast_add_fusion.9
  413.7 6.1 bitcast_add_fusion.9
  450.4 6.1 bitcast_add_fusion.9
  468.7 6.1 bitcast_add_fusion.9
  479.9 110.1 %while.83 = (s32[]{:T(128)}, f32[8,1,16,64]{3,2,0,1:T(8,128)S(1)}, f32[8,1,16,64]{3,2,0,1:T(8,128)S(1)}, f32[8,1,16,64,128]{4,3,2,0,1:T(8,128)}, s32[]{:T(128)},...) while((s32[]{:T(128)}, f32[8,1,16,64]{3,2,0,1:T(8,128)S(1)}, ...), condition=%wide.region_10.10_spmd.clone, body=%wide.region_7.9_spmd.clone.sunk | while | flops 550659712 | bytes 42241680 | solution.py:83
  489.7 6.1 bitcast_add_fusion.11
  508.0 6.1 bitcast_add_fusion.11
  526.4 6.1 bitcast_add_fusion.11
  544.7 6.1 bitcast_add_fusion.11
  563.1 6.1 bitcast_add_fusion.11
  581.4 6.1 bitcast_add_fusion.11
  596.0 53.9 %all_to_all.71 = bf16[1024,16,128]{2,1,0:T(8,128)(2,1)S(1)} all-to-all(bf16[1024,16,128]{2,1,0:T(8,128)(2,1)} %bitcast.29), channel_id=1, replica_groups=mesh['ctx'=16,'head'=8] {'head'}, dimensions={0} | all-to-all | bytes 8388608 | tf_op jit(solution)/shard_map/all_to_all | solution.py:135
  (711 shorter events, 355.8 us)
Async XLA Ops:
  6.5 92.5 %all-gather.3.cloned.1.call-start = ((), (), s32[]{:S(2)}) async-start(), calls=%async_computation.4 | async-start | bytes 4456448 | tf_op jit(solution)/shard_map/all_gather | solution.py:107
  19.3 104.1 %all-gather.5.cloned.1.call-start = ((), (), s32[]{:S(2)}) async-start(), calls=%async_computation.5 | async-start | bytes 4456448 | tf_op jit(solution)/shard_map/all_gather | solution.py:108
  37.7 4.7 copy-start.4
  37.7 4.9 copy-start.5
  37.7 54.4 %all-to-all-start = ((bf16[128,128,128]{2,0,1:T(8,128)(2,1)}), bf16[128,128,128]{2,0,1:T(8,128)(2,1)}, u32[]{:S(2)}, u32[]{:S(2)}) async-start(bf16[128,128,128]{2,0,1:T(8,128)(2,1)} %copy.86), calls=%async_computation | async-start | bytes 8388608 | tf_op jit(solution)/shard_map/all_to_all | solution.py:102
  92.1 31.3 %copy-start.2 = (s32[1,256]{1,0:T(1,128)S(1)}, s32[1,256]{1,0:T(1,128)}, u32[]{:S(2)}) copy-start(s32[1,256]{1,0:T(1,128)} %param.17) | copy-start | bytes 3076
  92.1 31.3 %copy-start.3 = (s32[1,256]{1,0:T(1,128)S(1)}, s32[1,256]{1,0:T(1,128)}, u32[]{:S(2)}) copy-start(s32[1,256]{1,0:T(1,128)} %param.19) | copy-start | bytes 3076
  140.7 6.1 copy-start
  159.0 6.1 copy-start
  177.4 6.1 copy-start
  195.7 6.1 copy-start
  214.1 6.1 copy-start
  232.4 6.1 copy-start
  253.4 6.1 copy-start.1
  271.7 6.1 copy-start.1
  290.1 6.1 copy-start.1
  308.4 6.1 copy-start.1
  326.8 6.1 copy-start.1
  345.1 6.1 copy-start.1
  376.9 6.1 copy-start
  395.3 6.1 copy-start
  413.7 6.1 copy-start
  432.0 6.1 copy-start
  450.4 6.1 copy-start
  468.7 6.1 copy-start
  489.7 6.1 copy-start.1
  508.0 6.1 copy-start.1
  526.4 6.1 copy-start.1
  544.7 6.1 copy-start.1
  563.1 6.1 copy-start.1
  581.4 6.1 copy-start.1
Sparse Core Ops, SparseCore 0:
  19.4 50.7 all-gather.2
  72.3 51.0 all-gather.4
where the time goes:
time: 662 us; the launch traced here: 660 us
  matrix products  222 us (34%)
  local copies, waits for them, and re-layouts  190 us (29%)
  blocking collectives  76.2 us (12%)
  other arithmetic  74.9 us (11%)
  waiting for transfers between devices  73.8 us (11%)
  between operations  13.4 us (2%)
    dot_general x24, matrix products, visit(): jnp.einsum('bngqs,bnsd->bngqd', probs.astype(jnp.bfloat16), value_tiles,...  147 us
    dot_general x24, matrix products, visit(): jnp.einsum('bqngd,bnsd->bngqs', query_group, key_tiles, preferred_element...  75.1 us
    gather x24, local copies, waits for them, and re-layouts, visit(): key_table[blocks, :, head_lanes]  66.9 us
    gather x24, local copies, waits for them, and re-layouts, visit(): value_table[blocks, :, head_lanes]  66.9 us
    reduce_sum x24, other arithmetic, visit(): totals = totals * decay_old + jnp.sum(probs, axis=-1)  57.2 us
    all_to_all x1, blocking collectives, on_device(): lax.all_to_all(answers, 'head', split_axis=0, concat_axis=1, tiled=True)  53.9 us
    all_to_all x1, waiting for transfers between devices, on_device(): lax.all_to_all(query_states, 'head', split_axis=1, concat_axis=0, tiled=T...  49.4 us
    all_gather x1, waiting for transfers between devices, on_device(): lax.all_gather(value_local, 'ctx', axis=0, tiled=True)  24.4 us
  transfers between devices with their start and end apart: 3, of which 2 were waited for; matrix products, arithmetic and copies ran while one was open for 2% of the time, Pallas kernels for 0%

commit v1 on v0

v1 whole, which is shorter than its diff:
```python
import functools
import math

import jax
import jax.numpy as jnp
from jax import lax
from jax.experimental import pallas as pl
from jax.experimental.pallas import tpu as pltpu
from jax.sharding import PartitionSpec as P

BLK = 64
G = 16
NS = 12
NV = 12
HD = 128
SLOTS = NS + NV
KEYS = SLOTS * BLK
ROWS = 512
NEG = -1e30
FACTOR = HD ** -0.5 * math.log2(math.e)


def attention_kernel(
    so_ref, sc_ref, vb_ref, vc_ref, q_ref, k_ref, v_ref, o_ref, kg, vg, scores, tops
):
    blocks = q_ref.shape[0]
    first = lax.axis_index("ctx") * blocks

    def fetch(i, side):
        b = first + i
        slash_live = sc_ref[0, b]
        vertical_live = vc_ref[0, b]
        for j in range(SLOTS):
            if j < NS:
                block = b - so_ref[0, b, j]
                live = j < slash_live
            else:
                block = vb_ref[0, b, j - NS]
                live = j - NS < vertical_live
            here = pl.ds(j * BLK, BLK)
            kg[side, here, :HD] = k_ref[block]
            bias = jnp.where(live, 0.0, NEG).astype(jnp.float32)
            kg[side, here, HD:] = jnp.full((BLK, HD), bias, jnp.float32).astype(jnp.bfloat16)
            vg[side, here, :HD] = v_ref[block]

    def score(i, half, side):
        tokens = ROWS // G
        queries = q_ref[i, pl.ds(half * tokens, tokens)].reshape(ROWS, HD)
        pick = (lax.broadcasted_iota(jnp.int32, (ROWS, HD), 1) == 0).astype(jnp.bfloat16)
        lhs = jnp.concatenate([queries, pick], axis=1)
        got = lax.dot_general(
            lhs, kg[side], (((1,), (1,)), ((), ())), preferred_element_type=jnp.float32
        )
        row = lax.broadcasted_iota(jnp.int32, (ROWS, 2 * BLK), 0) // G + half * tokens
        col = lax.broadcasted_iota(jnp.int32, (ROWS, 2 * BLK), 1)
        edge = jnp.where((col >= BLK) | (col <= row), got[:, : 2 * BLK], NEG)
        scores[half, :, : 2 * BLK] = edge
        scores[half, :, 2 * BLK :] = got[:, 2 * BLK :]
        top = jnp.maximum(
            jnp.max(edge, axis=1, keepdims=True), jnp.max(got[:, 2 * BLK :], axis=1, keepdims=True)
        )
        tops[half] = jnp.broadcast_to(top * FACTOR, (ROWS, HD))

    def answer(i, half, side):
        tokens = ROWS // G
        top = jnp.concatenate([tops[half]] * (KEYS // HD), axis=1)
        probs = jnp.exp2(scores[half] * FACTOR - top).astype(jnp.bfloat16)
        got = jnp.dot(probs, vg[side], preferred_element_type=jnp.float32)
        out = (got[:, :HD] / got[:, HD:]).astype(jnp.bfloat16)
        o_ref[i, pl.ds(half * tokens, tokens)] = out.reshape(tokens, G, HD)

    vg[:, :, HD:] = jnp.ones((2, KEYS, HD), jnp.bfloat16)
    fetch(0, 0)
    score(0, 0, 0)

    def step(i, carry):
        side = lax.rem(i, 2)
        score(i, 1, side)
        answer(i, 0, side)
        later = jnp.minimum(i + 1, blocks - 1)
        fetch(later, 1 - side)
        score(later, 0, 1 - side)
        answer(i, 1, side)
        return carry

    lax.fori_loop(0, blocks, step, 0)


def attention(query, keys, values, so, sc, vb, vc):
    smem = pl.BlockSpec(memory_space=pltpu.SMEM)
    vmem = pl.BlockSpec(memory_space=pltpu.VMEM)
    return pl.pallas_call(
        attention_kernel,
        out_shape=jax.ShapeDtypeStruct(query.shape, query.dtype),
        in_specs=[smem] * 4 + [vmem] * 3,
        out_specs=vmem,
        scratch_shapes=[
            pltpu.VMEM((2, KEYS, 2 * HD), jnp.bfloat16),
            pltpu.VMEM((2, KEYS, 2 * HD), jnp.bfloat16),
            pltpu.VMEM((2, ROWS, KEYS), jnp.float32),
            pltpu.VMEM((2, ROWS, HD), jnp.float32),
        ],
        compiler_params=pltpu.CompilerParams(vmem_limit_bytes=60 << 20),
    )(so, sc, vb, vc, query, keys, values)


def on_device(query_states, key_states, value_states, so, sc, vb, vc):
    def exchange(x):
        return lax.all_to_all(x, "head", split_axis=1, concat_axis=0, tiled=True)

    key_local, value_local = exchange(key_states), exchange(value_states)
    key_full = lax.all_gather(key_local, "ctx", axis=0, tiled=True)
    value_full = lax.all_gather(value_local, "ctx", axis=0, tiled=True)
    query_local = exchange(query_states)
    rows = query_local.shape[0]
    answers = attention(
        query_local.reshape(rows // BLK, BLK, G, HD),
        key_full.reshape(-1, BLK, HD),
        value_full.reshape(-1, BLK, HD),
        so, sc, vb, vc,
    )
    return lax.all_to_all(
        answers.reshape(rows, G, HD), "head", split_axis=0, concat_axis=1, tiled=True
    )


def solution(mesh):
    token = P(("ctx", "head"), None, None)
    in_specs = (token,) * 3 + (P("head", None, None), P("head", None)) * 2
    return jax.shard_map(
        on_device, mesh=mesh, in_specs=in_specs, out_specs=token, check_vma=False
    )
```

time: 662 us -> 231 us (0.35)
  the two profiles are of different devices: /device:TPU:96 before, /device:TPU:1 now
where the time goes in v1:
time: 231 us; the launch traced here: 230 us
  blocking collectives  76.5 us (33%)
  waiting for transfers between devices  72.9 us (32%)
  Pallas kernels  40.8 us (18%)
  local copies, waits for them, and re-layouts  20.7 us (9%)
  between operations  13.4 us (6%)
  starting transfers between devices  5.65 us (2%)
    all_to_all x1, blocking collectives, on_device(): lax.all_to_all(answers.reshape(rows, G, HD), 'head', split_axis=0, concat...  53.7 us
    all_to_all x1, waiting for transfers between devices, exchange(): return lax.all_to_all(x, 'head', split_axis=1, concat_axis=0, tiled=True)  47.3 us
    pallas_call x1, Pallas kernels, attention(): pl.pallas_call(attention_kernel, out_shape=jax.ShapeDtypeStruct(query.sha...  40.8 us
    all_gather x1, waiting for transfers between devices, on_device(): key_full = lax.all_gather(key_local, 'ctx', axis=0, tiled=True)  25.6 us
    all_to_all x2, blocking collectives, exchange(): return lax.all_to_all(x, 'head', split_axis=1, concat_axis=0, tiled=True)  22.7 us
    unnamed x9, local copies, waits for them, and re-layouts  10.5 us
    all_to_all x1, local copies, waits for them, and re-layouts, exchange(): return lax.all_to_all(x, 'head', split_axis=1, concat_axis=0, tiled=True)  6.98 us
    all_to_all x1, starting transfers between devices, exchange(): return lax.all_to_all(x, 'head', split_axis=1, concat_axis=0, tiled=True)  5.61 us
  transfers between devices with their start and end apart: 3, of which 2 were waited for; matrix products, arithmetic and copies ran while one was open for 7% of the time, Pallas kernels for 0%

profile of v1, /device:TPU:1, one launch (start us, length us, event | category | flops | bytes accessed | tf_op | source)
XLA Modules:
  0.0 230.0 jit_solution(5394000236391355755)
XLA Ops:
  6.5 0.0 all-gather.5.cloned.1.call-start
  6.5 1.0 copy.21
  7.5 12.2 %all_to_all.69 = bf16[128,8,128]{2,0,1:T(8,128)(2,1)} all-to-all(bf16[128,8,128]{2,0,1:T(8,128)(2,1)S(1)} %copy.21), channel_id=1, replica_groups=mesh['ctx'=16,'head'=8] {'head'}, dimensions={1} | all-to-all | bytes 524288 | tf_op jit(solution)/shard_map/all_to_all | solution.py:109
  19.7 0.0 all-gather.5.cloned.1.call-update
  19.7 0.0 all-gather.3.cloned.1.call-start
  19.8 1.0 copy.20
  20.8 10.6 %all_to_all.70 = bf16[128,8,128]{2,0,1:T(8,128)(2,1)} all-to-all(bf16[128,8,128]{2,0,1:T(8,128)(2,1)S(1)} %copy.20), channel_id=1, replica_groups=mesh['ctx'=16,'head'=8] {'head'}, dimensions={1} | all-to-all | bytes 524288 | tf_op jit(solution)/shard_map/all_to_all | solution.py:109
  31.3 0.0 all-gather.3.cloned.1.call-update
  31.4 6.9 %copy.18 = bf16[128,128,128]{2,0,1:T(8,128)(2,1)} copy(bf16[128,128,128]{2,1,0:T(8,128)(2,1)} %param.7) | data formatting | bytes 8388608 | tf_op args[0]
  38.3 0.0 copy-start
  38.3 0.0 copy-start.1
  38.3 5.6 %all-to-all-start = ((bf16[128,128,128]{2,0,1:T(8,128)(2,1)}), bf16[128,128,128]{2,0,1:T(8,128)(2,1)}, u32[]{:S(2)}, u32[]{:S(2)}) async-start(bf16[128,128,128]{2,0,1:T(8,128)(2,1)} %copy.18), calls=%async_computation | async-start | bytes 8388608 | tf_op jit(solution)/shard_map/all_to_all | solution.py:109
  43.9 0.0 copy-done
  43.9 0.8 copy.22.so_ref
  44.7 0.0 copy-done.1
  44.7 0.8 copy.23.vb_ref
  45.5 47.3 %all-to-all-done = bf16[128,128,128]{2,0,1:T(8,128)(2,1)} async-done(((bf16[128,128,128]{2,0,1:T(8,128)(2,1)}), bf16[128,128,128]{2,0,1:T(8,128)(2,1)}, u32[]{:S(2)}, u32[]{:S(2)}) %all-to-all-start) | async-done | bytes 4194336 | tf_op jit(solution)/shard_map/all_to_all | solution.py:109
  92.7 7.0 %copy.19 = bf16[128,8,16,128]{3,2,0,1:T(8,128)(2,1)} copy(bf16[128,8,16,128]{3,0,2,1:T(8,128)(2,1)} %bitcast) | data formatting | bytes 8388608 | tf_op jit(solution)/shard_map/all_to_all | solution.py:109
  99.7 0.0 all-gather.5.cloned.1.call-done
  99.7 25.6 %all-gather.3.cloned.1.call-done = bf16[16384,1,128]{2,0,1:T(8,128)(2,1)} async-done(((bf16[1024,1,128]{2,0,1:T(8,128)(2,1)}), bf16[16384,1,128]{2,0,1:T(8,128)(2,1)}) %all-gather.3.cloned.1.call-update) | async-done | bytes 4194320 | tf_op jit(solution)/shard_map/all_gather | solution.py:112
  125.3 40.8 %shard_map.73 = bf16[16,64,16,128]{3,2,1,0:T(8,128)(2,1)} custom-call(s32[1,256,12]{2,1,0:T(8,128)} %copy.22.so_ref, s32[1,256]{1,0:T(1,128)} %sc_ref.1, s32[1,256,12]{2,1,0:T(8,128)} %copy.23.vb_ref, s32[1,256]{1,0:T(1,128)} %vc_ref.1, bf16[16,64,16,128]{3,2,1,0:T(8,128)(2,1)} %bitcast.21, bf16[256,64,128]{2,1,0:T(8,128)(2,1)} %bitcast.25, ...), custom_call_target="tpu_custom_call" | custom-call | tf_op jit(solution)/shard_map/pallas_call | solution.py:92
  166.2 53.7 %all_to_all.71 = bf16[1024,16,128]{2,1,0:T(8,128)(2,1)S(1)} all-to-all(bf16[1024,16,128]{2,1,0:T(8,128)(2,1)} %bitcast.22), channel_id=1, replica_groups=mesh['ctx'=16,'head'=8] {'head'}, dimensions={0} | all-to-all | bytes 8388608 | tf_op jit(solution)/shard_map/all_to_all | solution.py:122
  219.9 3.3 %copy.24 = bf16[8,128,16,128]{3,2,0,1:T(8,128)(2,1)} copy(bf16[8,128,16,128]{3,2,1,0:T(8,128)(2,1)S(1)} %bitcast.23) | data formatting | bytes 8388608 | tf_op jit(solution)/shard_map/all_to_all | solution.py:122
Async XLA Ops:
  6.5 93.2 %all-gather.5.cloned.1.call-start = ((), (), s32[]{:S(2)}) async-start(), calls=%async_computation.5 | async-start | bytes 4456448 | tf_op jit(solution)/shard_map/all_gather | solution.py:113
  19.7 105.6 %all-gather.3.cloned.1.call-start = ((), (), s32[]{:S(2)}) async-start(), calls=%async_computation.4 | async-start | bytes 4456448 | tf_op jit(solution)/shard_map/all_gather | solution.py:112
  38.3 5.6 %copy-start = (s32[1,256,12]{1,0,2:T(1,128)S(1)}, s32[1,256,12]{1,0,2:T(1,128)}, u32[]{:S(2)}) copy-start(s32[1,256,12]{1,0,2:T(1,128)} %param.10) | copy-start | bytes 36868
  38.3 6.4 %copy-start.1 = (s32[1,256,12]{1,0,2:T(1,128)S(1)}, s32[1,256,12]{1,0,2:T(1,128)}, u32[]{:S(2)}) copy-start(s32[1,256,12]{1,0,2:T(1,128)} %param.12) | copy-start | bytes 36868
  38.3 54.4 %all-to-all-start = ((bf16[128,128,128]{2,0,1:T(8,128)(2,1)}), bf16[128,128,128]{2,0,1:T(8,128)(2,1)}, u32[]{:S(2)}, u32[]{:S(2)}) async-start(bf16[128,128,128]{2,0,1:T(8,128)(2,1)} %copy.18), calls=%async_computation | async-start | bytes 8388608 | tf_op jit(solution)/shard_map/all_to_all | solution.py:109
Sparse Core Ops, SparseCore 0:
  19.8 52.2 all-gather.4
  74.2 51.0 all-gather.2

commit v2 on v1

v2 whole, which is shorter than its diff:
```python
import math

import jax
import jax.numpy as jnp
from jax import lax
from jax.experimental import pallas as pl
from jax.experimental.pallas import tpu as pltpu
from jax.sharding import PartitionSpec as P

BLK = 64
G = 16
NS = 12
NV = 12
HD = 128
SLOTS = NS + NV
KEYS = SLOTS * BLK
ROWS = 512
RING = 4
HEADS = 2 * RING
SHARD = 2 * HEADS
BLOCKS = RING * RING * SHARD
NEG = -1e30
FACTOR = HD ** -0.5 * math.log2(math.e)
MESH = pl.DeviceIdType.MESH
PARTNERS = ((2, 0), (2, 1), (1, 0), (3, 0), (1, 1), (3, 1), (0, 1), (0, 0))


def remote(src, dst, send, recv, device):
    return pltpu.make_async_remote_copy(
        src_ref=src, dst_ref=dst, send_sem=send, recv_sem=recv, device_id=device, device_id_type=MESH
    )


def kernel(
    so_ref, sc_ref, vb_ref, vc_ref, q_ref, kv_ref, o_ref,
    qs, kv, os, kg, vg, scores, tops,
    q_send, q_recv, kv_send, kv_recv, o_send, o_recv,
):
    me, head = lax.axis_index("ctx"), lax.axis_index("head")
    z, y = lax.div(me, RING), lax.rem(me, RING)
    x, core = lax.div(head, 2), lax.rem(head, 2)

    def place(dz, dy):
        return lax.rem(z + dz + RING, RING) * RING + lax.rem(y + dy + RING, RING)

    def partner(dx, other):
        return lax.rem(x + dx, RING) * 2 + lax.rem(core + other, 2)

    peers = [(me, partner(dx, other)) for dx, other in PARTNERS[:-1]]
    peers += [(place(0, 1), head), (place(0, -1), head), (place(1, 0), head), (place(-1, 0), head)]
    barrier = pltpu.get_barrier_semaphore()
    for peer in peers:
        pl.semaphore_signal(barrier, inc=1, device_id=peer, device_id_type=MESH)
    pl.semaphore_wait(barrier, len(peers))

    mine = pl.ds(me * SHARD + head * 2, 2)
    sent = []
    entry = []
    for n, (dx, other) in enumerate(PARTNERS[:-1]):
        to = partner(dx, other)
        copy = remote(kv_ref.at[to], kv.at[:, mine], kv_send.at[n], kv_recv.at[n], (me, to))
        copy.start()
        entry.append(copy)
    queries = []
    for n, (dx, other) in enumerate(PARTNERS[:-1]):
        to = partner(dx, other)
        copy = remote(
            q_ref.at[:, pl.ds(pl.multiple_of(to * G, G), G)], qs.at[head],
            q_send.at[n], q_recv.at[n], (me, to),
        )
        copy.start()
        queries.append(copy)
    own_q = pltpu.make_async_copy(
        q_ref.at[:, pl.ds(pl.multiple_of(head * G, G), G)], qs.at[head], q_send.at[7]
    )
    own_q.start()
    own_kv = pltpu.make_async_copy(kv_ref.at[head], kv.at[:, mine], kv_send.at[7])
    own_kv.start()
    own_kv.wait()
    for copy in entry:
        copy.wait_recv()
    sent += entry

    count = len(PARTNERS)

    def pass_on(which, shard, low, length, device):
        nonlocal count
        piece = kv.at[which, pl.ds(shard * SHARD + low, length)]
        copy = remote(piece, piece, kv_send.at[count], kv_recv.at[count], device)
        count += 1
        copy.start()
        sent.append(copy)
        return copy

    def at(which, first, second):
        return place(second, first) if which == 0 else place(first, second)

    half = SHARD // 2
    first = {}
    second = {}
    for which in (0, 1):
        for d in (1, -1):
            first[which, d] = pass_on(which, me, 0, SHARD, (at(which, d, 0), head))
    for which in (0, 1):
        for d in (1, -1):
            second[which, 0, d] = pass_on(which, me, 0, SHARD, (at(which, 0, d), head))
    first_far = []
    for d in (1, -1):
        for which in (0, 1):
            first[which, d].wait_recv()
            shard = at(which, -d, 0)
            low = 0 if d == 1 else half
            first_far.append(pass_on(which, shard, low, half, (at(which, d, 0), head)))
            for e in (1, -1):
                second[which, -d, e] = pass_on(which, shard, 0, SHARD, (at(which, 0, e), head))
    second_far = []

    def relay(line):
        for which in (0, 1):
            for e in (1, -1):
                second[which, line, e].wait_recv()
                low = 0 if e == 1 else half
                second_far.append(
                    pass_on(which, at(which, line, -e), low, half, (at(which, 0, e), head))
                )

    relay(0)
    for copy in first_far:
        copy.wait_recv()
    for which in (0, 1):
        for e in (1, -1):
            second[which, 2, e] = pass_on(which, at(which, 2, 0), 0, SHARD, (at(which, 0, e), head))
    for line in (-1, 1, 2):
        relay(line)
    for copy in second_far:
        copy.wait_recv()
    for copy in queries:
        copy.wait_recv()
    own_q.wait()

    def turn(i):
        n = lax.div(i, 2)
        dx = jnp.where(n < 2, 2, jnp.where(n < 6, 1 + 2 * lax.rem(n, 2), 0))
        other = jnp.where((n == 1) | ((n >= 4) & (n <= 6)), 1, 0)
        return partner(dx, other), lax.rem(i, 2)

    def fetch(i, side):
        source, part = turn(i)
        b = me * SHARD + source * 2 + part
        slash_live = sc_ref[0, b]
        vertical_live = vc_ref[0, b]
        for j in range(SLOTS):
            if j < NS:
                block = b - so_ref[0, b, j]
                live = j < slash_live
            else:
                block = vb_ref[0, b, j - NS]
                live = j - NS < vertical_live
            here = pl.ds(j * BLK, BLK)
            kg[side, here, :HD] = kv[0, block]
            bias = jnp.where(live, 0.0, NEG).astype(jnp.float32)
            kg[side, here, HD:] = jnp.full((BLK, HD), bias, jnp.float32).astype(jnp.bfloat16)
            vg[side, here, :HD] = kv[1, block]

    tokens = ROWS // G

    def score(i, half, side):
        source, part = turn(i)
        rows = qs[source, pl.ds(part * BLK + half * tokens, tokens)].reshape(ROWS, HD)
        pick = (lax.broadcasted_iota(jnp.int32, (ROWS, HD), 1) == 0).astype(jnp.bfloat16)
        lhs = jnp.concatenate([rows, pick], axis=1)
        got = lax.dot_general(
            lhs, kg[side], (((1,), (1,)), ((), ())), preferred_element_type=jnp.float32
        )
        row = lax.broadcasted_iota(jnp.int32, (ROWS, 2 * BLK), 0) // G + half * tokens
        col = lax.broadcasted_iota(jnp.int32, (ROWS, 2 * BLK), 1)
        edge = jnp.where((col >= BLK) | (col <= row), got[:, : 2 * BLK], NEG)
        scores[half, :, : 2 * BLK] = edge
        scores[half, :, 2 * BLK :] = got[:, 2 * BLK :]
        top = jnp.maximum(
            jnp.max(edge, axis=1, keepdims=True), jnp.max(got[:, 2 * BLK :], axis=1, keepdims=True)
        )
        tops[half] = jnp.broadcast_to(top * FACTOR, (ROWS, HD))

    def answer(i, half, side):
        source, part = turn(i)
        top = jnp.concatenate([tops[half]] * (KEYS // HD), axis=1)
        probs = jnp.exp2(scores[half] * FACTOR - top).astype(jnp.bfloat16)
        got = jnp.dot(probs, vg[side], preferred_element_type=jnp.float32)
        out = (got[:, :HD] / got[:, HD:]).astype(jnp.bfloat16)
        os[source, pl.ds(part * BLK + half * tokens, tokens)] = out.reshape(tokens, G, HD)

    columns = pl.ds(pl.multiple_of(head * G, G), G)

    def give(i):
        source, part = turn(i)
        rows = pl.ds(part * BLK, BLK)
        return remote(
            os.at[source, rows], o_ref.at[rows, columns], o_send.at[i], o_recv.at[i], (me, source)
        )

    def keep(part):
        rows = pl.ds(part * BLK, BLK)
        return pltpu.make_async_copy(
            os.at[head, rows], o_ref.at[rows, columns], o_send.at[SHARD - 2 + part]
        )

    vg[:, :, HD:] = jnp.ones((2, KEYS, HD), jnp.bfloat16)
    fetch(0, 0)
    score(0, 0, 0)

    def step(i, carry):
        side = lax.rem(i, 2)
        score(i, 1, side)

        @pl.when((i >= 1) & (i <= SHARD - 2))
        def _():
            give(i - 1).start()

        answer(i, 0, side)
        later = jnp.minimum(i + 1, SHARD - 1)
        fetch(later, 1 - side)
        score(later, 0, 1 - side)
        answer(i, 1, side)
        return carry

    lax.fori_loop(0, SHARD, step, 0)
    for part in range(2):
        keep(part).start()
    for copy in sent + queries:
        copy.wait_send()
    for part in range(2):
        keep(part).wait()

    def finish(i, carry):
        give(i).wait()
        return carry

    lax.fori_loop(0, SHARD - 2, finish, 0)


def on_device(query_states, key_states, value_states, so, sc, vb, vc):
    rows = query_states.shape[0]

    def by_head(a):
        return jnp.transpose(a, (1, 0, 2)).reshape(HEADS, 1, rows // BLK, BLK, HD)

    kv = jnp.concatenate([by_head(key_states), by_head(value_states)], axis=1)
    smem = pl.BlockSpec(memory_space=pltpu.SMEM)
    hbm = pl.BlockSpec(memory_space=pl.ANY)
    bf16 = jnp.bfloat16
    return pl.pallas_call(
        kernel,
        out_shape=jax.ShapeDtypeStruct(query_states.shape, query_states.dtype),
        in_specs=[smem] * 4 + [hbm] * 2,
        out_specs=hbm,
        scratch_shapes=[
            pltpu.VMEM((HEADS, 2 * BLK, G, HD), bf16),
            pltpu.VMEM((2, BLOCKS, BLK, HD), bf16),
            pltpu.VMEM((HEADS, 2 * BLK, G, HD), bf16),
            pltpu.VMEM((2, KEYS, 2 * HD), bf16),
            pltpu.VMEM((2, KEYS, 2 * HD), bf16),
            pltpu.VMEM((2, ROWS, KEYS), jnp.float32),
            pltpu.VMEM((2, ROWS, HD), jnp.float32),
            pltpu.SemaphoreType.DMA((8,)),
            pltpu.SemaphoreType.DMA((8,)),
            pltpu.SemaphoreType.DMA((48,)),
            pltpu.SemaphoreType.DMA((48,)),
            pltpu.SemaphoreType.DMA((SHARD,)),
            pltpu.SemaphoreType.DMA((SHARD,)),
        ],
        compiler_params=pltpu.CompilerParams(
            collective_id=0, has_side_effects=True, vmem_limit_bytes=60 << 20
        ),
    )(so, sc, vb, vc, query_states, kv)


def solution(mesh):
    token = P(("ctx", "head"), None, None)
    in_specs = (token,) * 3 + (P("head", None, None), P("head", None)) * 2
    return jax.shard_map(
        on_device, mesh=mesh, in_specs=in_specs, out_specs=token, check_vma=False
    )
```

time: 231 us -> 136 us (0.59)
  Pallas kernels: 40.8 us -> 125 us
  blocking collectives: 76.5 us -> 0 us
  waiting for transfers between devices: 72.9 us -> 0 us
  between operations: 13.4 us -> 0.02 us
  local copies, waits for them, and re-layouts: 20.7 us -> 9.67 us
  starting transfers between devices: 5.65 us -> 0 us
    pallas_call x1, Pallas kernels: 40.8 us -> 125 us  [on_device(): pl.pallas_call(kernel, out_shape=jax.ShapeDtypeStruct(query_states.shape,...]
    all_to_all x3 -> x0, blocking collectives: 76.5 us -> none  [the longest x1 53.7 us: on_device(): lax.all_to_all(answers.reshape(rows, G, HD), 'head', split_axis=0, concat...]
    all_to_all x1 -> x0, waiting for transfers between devices: 47.3 us -> none  [exchange(): return lax.all_to_all(x, 'head', split_axis=1, concat_axis=0, tiled=True)]
    all_gather x2 -> x0, waiting for transfers between devices: 25.6 us -> none  [the longest x1 25.6 us: on_device(): key_full = lax.all_gather(key_local, 'ctx', axis=0, tiled=True)]
    all_to_all x2 -> x0, local copies, waits for them, and re-layouts: 10.2 us -> none  [the longest x1 6.98 us: exchange(): return lax.all_to_all(x, 'head', split_axis=1, concat_axis=0, tiled=True)]
    all_to_all x1 -> x0, starting transfers between devices: 5.61 us -> none  [exchange(): return lax.all_to_all(x, 'head', split_axis=1, concat_axis=0, tiled=True)]
    unnamed x9 -> x3, local copies, waits for them, and re-layouts: 10.5 us -> 7.7 us
  transfers between devices with their start and end apart: 3 -> 0, of which waited for: 2 -> 0; matrix products, arithmetic and copies ran while one was open for 7% -> 0% of each run, Pallas kernels for 0% -> 0%
where the time goes in v2:
time: 136 us
  Pallas kernels  125 us (92%)
  local copies, waits for them, and re-layouts  9.67 us (7%)
    pallas_call x1, Pallas kernels, on_device(): pl.pallas_call(kernel, out_shape=jax.ShapeDtypeStruct(query_states.shape,...  125 us
    unnamed x3, local copies, waits for them, and re-layouts  7.7 us

profile of v2, /device:TPU:1, one launch (start us, length us, event | category | flops | bytes accessed | tf_op | source)
XLA Modules:
  0.0 135.8 jit_solution(2497152748168575344)
XLA Ops:
  0.0 1.5 %copy.10.so_ref = s32[1,256,12]{2,1,0:T(8,128)} copy(s32[1,256,12]{1,0,2:T(1,128)} %param.10) | data formatting | bytes 24576 | tf_op args[3]
  1.5 1.5 %copy.11.vb_ref = s32[1,256,12]{2,1,0:T(8,128)} copy(s32[1,256,12]{1,0,2:T(1,128)} %param.12) | data formatting | bytes 24576 | tf_op args[5]
  2.9 1.0 copy.8
  3.9 1.0 copy.9
  4.9 0.8 pad_maximum_fusion.kv_ref
  5.7 125.2 %shard_map.73 = bf16[128,128,128]{2,1,0:T(8,128)(2,1)} custom-call(s32[1,256,12]{2,1,0:T(8,128)} %copy.10.so_ref, s32[1,256]{1,0:T(1,128)} %sc_ref.1, s32[1,256,12]{2,1,0:T(8,128)} %copy.11.vb_ref, s32[1,256]{1,0:T(1,128)} %vc_ref.1, bf16[128,128,128]{2,1,0:T(8,128)(2,1)} %q_ref.1, bf16[8,2,2,64,128]{4,3,2,1,0:T(8,128)(2,1)} %pad_maximum_fusion.kv_ref), custom_call_target="tpu_custom_call" | custom-call | tf_op jit(solution)/shard_map/pallas_call | solution.py:252
  131.0 4.8 %copy.13 = bf16[128,128,128]{2,1,0:T(8,128)(2,1)} copy(bf16[128,128,128]{2,1,0:T(8,128)(2,1)} %shard_map.73) | data formatting | bytes 8388608

commit v3 on v2

--- a/solution.py
+++ b/solution.py
@@ -32,13 +32,22 @@
 
 
 def kernel(
-    so_ref, sc_ref, vb_ref, vc_ref, q_ref, kv_ref, o_ref,
-    qs, kv, os, kg, vg, scores, tops,
-    q_send, q_recv, kv_send, kv_recv, o_send, o_recv,
+    so_hbm, sc_hbm, vb_hbm, vc_hbm, q_ref, k_hbm, v_hbm, o_ref,
+    so_ref, sc_ref, vb_ref, vc_ref, k_ref, v_ref, kv_ref, qs, kv, os, kg, vg, scores, tops,
+    q_send, q_recv, kv_send, kv_recv, o_send, o_recv, local,
 ):
     me, head = lax.axis_index("ctx"), lax.axis_index("head")
     z, y = lax.div(me, RING), lax.rem(me, RING)
     x, core = lax.div(head, 2), lax.rem(head, 2)
+
+    tables = [
+        pltpu.make_async_copy(src, dst, local.at[n])
+        for n, (src, dst) in enumerate(
+            ((k_hbm, k_ref), (v_hbm, v_ref), (so_hbm, so_ref), (sc_hbm, sc_ref), (vb_hbm, vb_ref), (vc_hbm, vc_ref))
+        )
+    ]
+    for copy in tables:
+        copy.start()
 
     def place(dz, dy):
         return lax.rem(z + dz + RING, RING) * RING + lax.rem(y + dy + RING, RING)
@@ -51,6 +60,11 @@
     barrier = pltpu.get_barrier_semaphore()
     for peer in peers:
         pl.semaphore_signal(barrier, inc=1, device_id=peer, device_id_type=MESH)
+    for copy in tables[:2]:
+        copy.wait()
+    for which, ref in ((0, k_ref), (1, v_ref)):
+        for n in range(HEADS):
+            kv_ref[n, which] = ref[:, n, :].reshape(2, BLK, HD)
     pl.semaphore_wait(barrier, len(peers))
 
     mine = pl.ds(me * SHARD + head * 2, 2)
@@ -137,6 +151,8 @@
     for copy in queries:
         copy.wait_recv()
     own_q.wait()
+    for copy in tables[2:]:
+        copy.wait()
 
     def turn(i):
         n = lax.div(i, 2)
@@ -151,10 +167,10 @@
         vertical_live = vc_ref[0, b]
         for j in range(SLOTS):
             if j < NS:
-                block = b - so_ref[0, b, j]
+                block = b - so_ref[j, 0, b]
                 live = j < slash_live
             else:
-                block = vb_ref[0, b, j - NS]
+                block = vb_ref[j - NS, 0, b]
                 live = j - NS < vertical_live
             here = pl.ds(j * BLK, BLK)
             kg[side, here, :HD] = kv[0, block]
@@ -240,21 +256,23 @@
 
 
 def on_device(query_states, key_states, value_states, so, sc, vb, vc):
-    rows = query_states.shape[0]
-
-    def by_head(a):
-        return jnp.transpose(a, (1, 0, 2)).reshape(HEADS, 1, rows // BLK, BLK, HD)
-
-    kv = jnp.concatenate([by_head(key_states), by_head(value_states)], axis=1)
-    smem = pl.BlockSpec(memory_space=pltpu.SMEM)
     hbm = pl.BlockSpec(memory_space=pl.ANY)
+    vmem = pl.BlockSpec(memory_space=pltpu.VMEM)
     bf16 = jnp.bfloat16
+    so, vb = jnp.transpose(so, (2, 0, 1)), jnp.transpose(vb, (2, 0, 1))
     return pl.pallas_call(
         kernel,
-        out_shape=jax.ShapeDtypeStruct(query_states.shape, query_states.dtype),
-        in_specs=[smem] * 4 + [hbm] * 2,
-        out_specs=hbm,
+        out_shape=pltpu.VMEM(query_states.shape, query_states.dtype),
+        in_specs=[hbm] * 7,
+        out_specs=vmem,
         scratch_shapes=[
+            pltpu.SMEM(so.shape, jnp.int32),
+            pltpu.SMEM(sc.shape, jnp.int32),
+            pltpu.SMEM(vb.shape, jnp.int32),
+            pltpu.SMEM(vc.shape, jnp.int32),
+            pltpu.VMEM(key_states.shape, bf16),
+            pltpu.VMEM(value_states.shape, bf16),
+            pltpu.VMEM((HEADS, 2, 2, BLK, HD), bf16),
             pltpu.VMEM((HEADS, 2 * BLK, G, HD), bf16),
             pltpu.VMEM((2, BLOCKS, BLK, HD), bf16),
             pltpu.VMEM((HEADS, 2 * BLK, G, HD), bf16),
@@ -268,11 +286,12 @@
             pltpu.SemaphoreType.DMA((48,)),
             pltpu.SemaphoreType.DMA((SHARD,)),
             pltpu.SemaphoreType.DMA((SHARD,)),
+            pltpu.SemaphoreType.DMA((6,)),
         ],
         compiler_params=pltpu.CompilerParams(
-            collective_id=0, has_side_effects=True, vmem_limit_bytes=60 << 20
+            collective_id=0, has_side_effects=True, vmem_limit_bytes=62_700_000
         ),
-    )(so, sc, vb, vc, query_states, kv)
+    )(so, sc, vb, vc, query_states, key_states, value_states)
 
 
 def solution(mesh):

time: 136 us -> 121 us (0.89)
  local copies, waits for them, and re-layouts: 9.67 us -> 2.02 us
  Pallas kernels: 125 us -> 119 us
    pallas_call x1, Pallas kernels: 125 us -> 119 us  [on_device(): pl.pallas_call(kernel, out_shape=pltpu.VMEM(query_states.shape, query_sta...]
    unnamed x3 -> x1, local copies, waits for them, and re-layouts: 7.7 us -> 2.02 us
    transpose x2 -> x0, local copies, waits for them, and re-layouts: 1.97 us -> none  [by_head(): return jnp.transpose(a, (1, 0, 2)).reshape(HEADS, 1, rows // BLK, BLK, HD)]
where the time goes in v3:
time: 121 us
  Pallas kernels  119 us (98%)
  local copies, waits for them, and re-layouts  2.02 us (2%)
    pallas_call x1, Pallas kernels, on_device(): pl.pallas_call(kernel, out_shape=pltpu.VMEM(query_states.shape, query_sta...  119 us

profile of v3, /device:TPU:1, one launch (start us, length us, event | category | flops | bytes accessed | tf_op | source)
XLA Modules:
  0.0 121.3 jit_solution(13037812411674552036)
XLA Ops:
  0.0 119.3 %shard_map.73 = bf16[128,128,128]{2,1,0:T(8,128)(2,1)S(1)} custom-call(s32[12,1,256]{2,1,0:T(1,128)} %bitcast.2, s32[1,256]{1,0:T(1,128)} %sc_hbm.1, s32[12,1,256]{2,1,0:T(1,128)} %bitcast.3, s32[1,256]{1,0:T(1,128)} %vc_hbm.1, bf16[128,128,128]{2,1,0:T(8,128)(2,1)} %q_ref.1, bf16[128,8,128]{2,1,0:T(8,128)(2,1)} %k_hbm.1, bf16[128,8,128]{2,1,0:T(8,128)(2,1)} %v_hbm.1), custom_call_target="tpu_custom_call" | custom-call | tf_op jit(solution)/shard_map/pallas_call | solution.py:263
  119.3 2.0 %copy.9 = bf16[128,128,128]{2,1,0:T(8,128)(2,1)} copy(bf16[128,128,128]{2,1,0:T(8,128)(2,1)S(1)} %shard_map.73) | data formatting | bytes 8388608

commit v4 on v3

v4 whole, which is shorter than its diff:
```python
import math

import jax
import jax.numpy as jnp
from jax import lax
from jax.experimental import pallas as pl
from jax.experimental.pallas import tpu as pltpu
from jax.sharding import PartitionSpec as P

BLK = 64
G = 16
NS = 12
NV = 12
HD = 128
SLOTS = NS + NV
KEYS = SLOTS * BLK
ROWS = 512
RING = 4
HEADS = 2 * RING
SHARD = 2 * HEADS
BLOCKS = RING * RING * SHARD
NEG = -1e30
FACTOR = HD ** -0.5 * math.log2(math.e)
MESH = pl.DeviceIdType.MESH
PARTNERS = ((2, 0), (2, 1), (1, 0), (3, 0), (1, 1), (3, 1), (0, 1), (0, 0))

STREAMS = ((0, 0, 16, True), (1, 0, 8, True), (1, 8, 8, False))
BATCHES = (2, 2, 2, 2, 2, 2)


def remote(src, dst, send, recv, device):
    return pltpu.make_async_remote_copy(
        src_ref=src, dst_ref=dst, send_sem=send, recv_sem=recv, device_id=device, device_id_type=MESH
    )


def kernel(
    so_hbm, sc_hbm, vb_hbm, vc_hbm, q_ref, k_hbm, v_hbm, o_ref,
    so_ref, sc_ref, vb_ref, vc_ref, so_in, sc_in, vb_in, vc_in, k_ref, v_ref, kv_ref, qs, kv, os, kg, vg, scores, tops,
    q_send, q_recv, kv_send, kv_recv, o_send, o_recv, local, t_send, t_recv,
):
    me, head = lax.axis_index("ctx"), lax.axis_index("head")
    z, y = lax.div(me, RING), lax.rem(me, RING)
    x, core = lax.div(head, 2), lax.rem(head, 2)

    def wrap(a):
        return lax.rem(a + RING, RING)

    def place(dz, dy):
        return wrap(z + dz) * RING + wrap(y + dy)

    def seat(dx, other):
        return wrap(x + dx) * 2 + lax.rem(core + other, 2)

    def served(d, other):
        return lax.rem(x + y + d + RING, RING) * 2 + lax.rem(core + other, 2)

    def partner(axis, d, other):
        return (me, seat(d, other)) if axis == 0 else (place(0, d), seat(0, other))

    def slant(d):
        return place(0, d), seat(-d, 0)

    loads = [
        pltpu.make_async_copy(src, dst, local.at[n])
        for n, (src, dst) in enumerate(((k_hbm, k_ref), (v_hbm, v_ref)))
    ]
    for copy in loads:
        copy.start()

    peers = [partner(0, d, other) for d, other in PARTNERS[:-1]]
    peers += [partner(1, d, other) for d, other in PARTNERS[:-2]]
    peers += [slant(1), slant(-1), (place(1, 0), head), (place(-1, 0), head)]
    barrier = pltpu.get_barrier_semaphore()
    for peer in peers:
        pl.semaphore_signal(barrier, inc=1, device_id=peer, device_id_type=MESH)
    for copy in loads:
        copy.wait()
    for which, ref in ((0, k_ref), (1, v_ref)):
        for n in range(HEADS):
            kv_ref[n, which] = ref[:, n, :].reshape(2, BLK, HD)
    pl.semaphore_wait(barrier, len(peers))

    mine = pl.ds(me * SHARD + head * 2, 2)
    sent = []
    entry = []
    for n, (d, other) in enumerate(PARTNERS[:-1]):
        copy = remote(
            kv_ref.at[served(d, other)], kv.at[:, mine], kv_send.at[n], kv_recv.at[n], partner(0, d, other)
        )
        copy.start()
        entry.append(copy)
    own_kv = pltpu.make_async_copy(kv_ref.at[served(0, 0)], kv.at[:, mine], kv_send.at[7])
    own_kv.start()
    tables = ((so_hbm, so_in, so_ref), (sc_hbm, sc_in, sc_ref), (vb_hbm, vb_in, vb_ref), (vc_hbm, vc_in, vc_ref))

    def here(n):
        return pltpu.make_async_copy(tables[n][0], tables[n][1], t_send.at[n])

    def there(n):
        return remote(tables[n][0], tables[n][1], t_send.at[4 + n], t_recv.at[n], (me, seat(-y, 0)))

    @pl.when(y == 0)
    def _():
        for n in range(4):
            here(n).start()

    @pl.when(y != 0)
    def _():
        for n in range(4):
            there(n).start()

    queries = []

    def ask(axis, n):
        d, other = PARTNERS[n]
        slot = axis * 8 + n
        copy = remote(
            q_ref.at[pl.ds(axis * BLK, BLK), pl.ds(pl.multiple_of(served(d, other) * G, G), G)], qs.at[slot],
            q_send.at[slot], q_recv.at[slot], partner(axis, d, other),
        )
        copy.start()
        queries.append(copy)

    own_q = []
    for axis in range(2):
        copy = pltpu.make_async_copy(
            q_ref.at[pl.ds(axis * BLK, BLK), pl.ds(pl.multiple_of(served(0, 0) * G, G), G)],
            qs.at[axis * 8 + 7], q_send.at[axis * 8 + 7],
        )
        copy.start()
        own_q.append(copy)
    asks = [(axis, n) for n in range(7) for axis in range(2)]

    def batch(size):
        for _ in range(min(size, len(asks))):
            ask(*asks.pop(0))

    batch(BATCHES[0])
    own_kv.wait()
    for copy in entry:
        copy.wait_recv()
    sent += entry

    count = len(PARTNERS)

    def pass_on(stream, shard, low, length, device):
        nonlocal count
        which, base, _, _ = stream
        piece = kv.at[which, pl.ds(shard * SHARD + base + low, length)]
        copy = remote(piece, piece, kv_send.at[count], kv_recv.at[count], device)
        count += 1
        copy.start()
        sent.append(copy)
        return copy

    def at(stream, one, two):
        return place(two, one) if stream[3] else place(one, two)

    def to(stream, ring, d):
        return slant(d) if stream[3] == (ring == 1) else (place(d, 0), head)

    first = {}
    second = {}
    for s in STREAMS:
        for d in (1, -1):
            first[s, d] = pass_on(s, me, 0, s[2], to(s, 1, d))
    for s in STREAMS:
        for d in (1, -1):
            second[s, 0, d] = pass_on(s, me, 0, s[2], to(s, 2, d))
    batch(BATCHES[1])
    first_far = []
    for d in (1, -1):
        for s in STREAMS:
            half = s[2] // 2
            first[s, d].wait_recv()
            shard = at(s, -d, 0)
            low = 0 if d == 1 else half
            first_far.append(pass_on(s, shard, low, half, to(s, 1, d)))
            for e in (1, -1):
                second[s, -d, e] = pass_on(s, shard, 0, s[2], to(s, 2, e))
    second_far = []

    def relay(line):
        for s in STREAMS:
            half = s[2] // 2
            for e in (1, -1):
                second[s, line, e].wait_recv()
                low = 0 if e == 1 else half
                second_far.append(pass_on(s, at(s, line, -e), low, half, to(s, 2, e)))

    batch(BATCHES[2])
    relay(0)
    for copy in first_far:
        copy.wait_recv()
    for s in STREAMS:
        for e in (1, -1):
            second[s, 2, e] = pass_on(s, at(s, 2, 0), 0, s[2], to(s, 2, e))
    batch(BATCHES[3])
    relay(-1)
    batch(BATCHES[4])
    relay(1)
    batch(BATCHES[5])
    relay(2)
    batch(14)

    @pl.when(y == 0)
    def _():
        for n in range(4):
            here(n).wait()

    @pl.when(y != 0)
    def _():
        for n in range(4):
            there(n).wait()

    index = [pltpu.make_async_copy(src, dst, local.at[2 + n]) for n, (_, src, dst) in enumerate(tables)]
    for copy in index:
        copy.start()
    for copy in index + own_q:
        copy.wait()
    for copy in second_far:
        copy.wait_recv()

    def turn(i):
        n = lax.div(i, 2)
        axis = lax.rem(i, 2)
        back = jnp.where(n < 2, 2, jnp.where(n < 6, 3 - 2 * lax.rem(n, 2), 0))
        other = jnp.where((n == 1) | ((n >= 4) & (n <= 6)), 1, 0)
        ctx = place(0, jnp.where(axis == 1, back, 0))
        return axis * 8 + n, axis, ctx, seat(jnp.where(axis == 0, back, 0), other)

    def fetch(i, side):
        _, axis, ctx, at_head = turn(i)
        b = ctx * SHARD + at_head * 2 + axis
        slash_live = sc_ref[0, b]
        vertical_live = vc_ref[0, b]
        for j in range(SLOTS):
            if j < NS:
                block = b - so_ref[j, 0, b]
                live = j < slash_live
            else:
                block = vb_ref[j - NS, 0, b]
                live = j - NS < vertical_live
            here = pl.ds(j * BLK, BLK)
            kg[side, here, :HD] = kv[0, block]
            bias = jnp.where(live, 0.0, NEG).astype(jnp.float32)
            kg[side, here, HD:] = jnp.full((BLK, HD), bias, jnp.float32).astype(jnp.bfloat16)
            vg[side, here, :HD] = kv[1, block]

    def arrive(i):
        @pl.when(i < SHARD - 2)
        def _():
            slot, _, ctx, at_head = turn(i)
            remote(qs.at[slot], qs.at[slot], q_send.at[slot], q_recv.at[slot], (ctx, at_head)).wait_recv()

    tokens = ROWS // G

    def score(i, half, side):
        rows = qs[turn(i)[0], pl.ds(half * tokens, tokens)].reshape(ROWS, HD)
        pick = (lax.broadcasted_iota(jnp.int32, (ROWS, HD), 1) == 0).astype(jnp.bfloat16)
        lhs = jnp.concatenate([rows, pick], axis=1)
        got = lax.dot_general(
            lhs, kg[side], (((1,), (1,)), ((), ())), preferred_element_type=jnp.float32
        )
        row = lax.broadcasted_iota(jnp.int32, (ROWS, 2 * BLK), 0) // G + half * tokens
        col = lax.broadcasted_iota(jnp.int32, (ROWS, 2 * BLK), 1)
        edge = jnp.where((col >= BLK) | (col <= row), got[:, : 2 * BLK], NEG)
        scores[half, :, : 2 * BLK] = edge
        scores[half, :, 2 * BLK :] = got[:, 2 * BLK :]
        top = jnp.maximum(
            jnp.max(edge, axis=1, keepdims=True), jnp.max(got[:, 2 * BLK :], axis=1, keepdims=True)
        )
        tops[half] = jnp.broadcast_to(top * FACTOR, (ROWS, HD))

    def answer(i, half, side):
        top = jnp.concatenate([tops[half]] * (KEYS // HD), axis=1)
        probs = jnp.exp2(scores[half] * FACTOR - top).astype(jnp.bfloat16)
        got = jnp.dot(probs, vg[side], preferred_element_type=jnp.float32)
        out = (got[:, :HD] / got[:, HD:]).astype(jnp.bfloat16)
        os[turn(i)[0], pl.ds(half * tokens, tokens)] = out.reshape(tokens, G, HD)

    columns = pl.ds(pl.multiple_of(served(0, 0) * G, G), G)

    def give(i):
        slot, axis, ctx, at_head = turn(i)
        rows = pl.ds(axis * BLK, BLK)
        return remote(
            os.at[slot], o_ref.at[rows, columns], o_send.at[slot], o_recv.at[slot], (ctx, at_head)
        )

    def keep(part):
        return pltpu.make_async_copy(
            os.at[part * 8 + 7], o_ref.at[pl.ds(part * BLK, BLK), columns], o_send.at[part * 8 + 7]
        )

    vg[:, :, HD:] = jnp.ones((2, KEYS, HD), jnp.bfloat16)
    fetch(0, 0)
    arrive(0)
    score(0, 0, 0)

    def step(i, carry):
        side = lax.rem(i, 2)
        later = jnp.minimum(i + 1, SHARD - 1)

        @pl.when((i >= 1) & (i <= SHARD - 2))
        def _():
            give(i - 1).start()

        arrive(i + 1)
        score(i, 1, side)
        answer(i, 0, side)
        fetch(later, 1 - side)
        score(later, 0, 1 - side)
        answer(i, 1, side)
        return carry

    lax.fori_loop(0, SHARD, step, 0)
    for part in range(2):
        keep(part).start()
    for copy in sent + queries:
        copy.wait_send()
    for part in range(2):
        keep(part).wait()

    def finish(i, carry):
        give(i).wait()
        return carry

    lax.fori_loop(0, SHARD - 2, finish, 0)


def on_device(query_states, key_states, value_states, so, sc, vb, vc):
    hbm = pl.BlockSpec(memory_space=pl.ANY)
    vmem = pl.BlockSpec(memory_space=pltpu.VMEM)
    bf16 = jnp.bfloat16
    so, vb = jnp.transpose(so, (2, 0, 1)), jnp.transpose(vb, (2, 0, 1))
    return pl.pallas_call(
        kernel,
        out_shape=pltpu.VMEM(query_states.shape, query_states.dtype),
        in_specs=[hbm] * 7,
        out_specs=vmem,
        scratch_shapes=[
            pltpu.SMEM(so.shape, jnp.int32),
            pltpu.SMEM(sc.shape, jnp.int32),
            pltpu.SMEM(vb.shape, jnp.int32),
            pltpu.SMEM(vc.shape, jnp.int32),
            pltpu.VMEM(so.shape, jnp.int32),
            pltpu.VMEM(sc.shape, jnp.int32),
            pltpu.VMEM(vb.shape, jnp.int32),
            pltpu.VMEM(vc.shape, jnp.int32),
            pltpu.VMEM(key_states.shape, bf16),
            pltpu.VMEM(value_states.shape, bf16),
            pltpu.VMEM((HEADS, 2, 2, BLK, HD), bf16),
            pltpu.VMEM((SHARD, BLK, G, HD), bf16),
            pltpu.VMEM((2, BLOCKS, BLK, HD), bf16),
            pltpu.VMEM((SHARD, BLK, G, HD), bf16),
            pltpu.VMEM((2, KEYS, 2 * HD), bf16),
            pltpu.VMEM((2, KEYS, 2 * HD), bf16),
            pltpu.VMEM((2, ROWS, KEYS), jnp.float32),
            pltpu.VMEM((2, ROWS, HD), jnp.float32),
            pltpu.SemaphoreType.DMA((SHARD,)),
            pltpu.SemaphoreType.DMA((SHARD,)),
            pltpu.SemaphoreType.DMA((8 + 20 * len(STREAMS),)),
            pltpu.SemaphoreType.DMA((8 + 20 * len(STREAMS),)),
            pltpu.SemaphoreType.DMA((SHARD,)),
            pltpu.SemaphoreType.DMA((SHARD,)),
            pltpu.SemaphoreType.DMA((6,)),
            pltpu.SemaphoreType.DMA((8,)),
            pltpu.SemaphoreType.DMA((4,)),
        ],
        compiler_params=pltpu.CompilerParams(
            collective_id=0, has_side_effects=True, vmem_limit_bytes=62_700_000
        ),
    )(so, sc, vb, vc, query_states, key_states, value_states)


def solution(mesh):
    token = P(("ctx", "head"), None, None)
    in_specs = (token,) * 3 + (P("head", None, None), P("head", None)) * 2
    return jax.shard_map(
        on_device, mesh=mesh, in_specs=in_specs, out_specs=token, check_vma=False
    )
```

time: 121 us -> 114 us (0.942); the launches traced: 121 us -> 113 us
  Pallas kernels: 119 us -> 111 us
    pallas_call x1, Pallas kernels: 119 us -> 111 us  [on_device(): pl.pallas_call(kernel, out_shape=pltpu.VMEM(query_states.shape, query_sta...]
where the time goes in v4:
time: 114 us; the launch traced here: 113 us
  Pallas kernels  111 us (97%)
  local copies, waits for them, and re-layouts  2.02 us (2%)
    pallas_call x1, Pallas kernels, on_device(): pl.pallas_call(kernel, out_shape=pltpu.VMEM(query_states.shape, query_sta...  111 us

profile of v4, /device:TPU:1, one launch (start us, length us, event | category | flops | bytes accessed | tf_op | source)
XLA Modules:
  0.0 113.1 jit_solution(16490776816057535681)
XLA Ops:
  0.0 111.1 %shard_map.73 = bf16[128,128,128]{2,1,0:T(8,128)(2,1)S(1)} custom-call(s32[12,1,256]{2,1,0:T(1,128)} %bitcast.2, s32[1,256]{1,0:T(1,128)} %sc_hbm.1, s32[12,1,256]{2,1,0:T(1,128)} %bitcast.3, s32[1,256]{1,0:T(1,128)} %vc_hbm.1, bf16[128,128,128]{2,1,0:T(8,128)(2,1)} %q_ref.1, bf16[128,8,128]{2,1,0:T(8,128)(2,1)} %k_hbm.1, bf16[128,8,128]{2,1,0:T(8,128)(2,1)} %v_hbm.1), custom_call_target="tpu_custom_call" | custom-call | tf_op jit(solution)/shard_map/pallas_call | solution.py:338
  111.1 2.0 %copy.9 = bf16[128,128,128]{2,1,0:T(8,128)(2,1)} copy(bf16[128,128,128]{2,1,0:T(8,128)(2,1)S(1)} %shard_map.73) | data formatting | bytes 8388608

commit v5 on v4

--- a/solution.py
+++ b/solution.py
@@ -25,7 +25,7 @@
 PARTNERS = ((2, 0), (2, 1), (1, 0), (3, 0), (1, 1), (3, 1), (0, 1), (0, 0))
 
 STREAMS = ((0, 0, 16, True), (1, 0, 8, True), (1, 8, 8, False))
-BATCHES = (2, 2, 2, 2, 2, 2)
+BATCHES = (0, 0, 2, 4, 4, 4)
 
 
 def remote(src, dst, send, recv, device):
@@ -168,6 +168,19 @@
     for s in STREAMS:
         for d in (1, -1):
             second[s, 0, d] = pass_on(s, me, 0, s[2], to(s, 2, d))
+    @pl.when(y == 0)
+    def _():
+        for n in range(4):
+            here(n).wait()
+
+    @pl.when(y != 0)
+    def _():
+        for n in range(4):
+            there(n).wait()
+
+    index = [pltpu.make_async_copy(src, dst, local.at[2 + n]) for n, (_, src, dst) in enumerate(tables)]
+    for copy in index:
+        copy.start()
     batch(BATCHES[1])
     first_far = []
     for d in (1, -1):
@@ -204,19 +217,6 @@
     relay(2)
     batch(14)
 
-    @pl.when(y == 0)
-    def _():
-        for n in range(4):
-            here(n).wait()
-
-    @pl.when(y != 0)
-    def _():
-        for n in range(4):
-            there(n).wait()
-
-    index = [pltpu.make_async_copy(src, dst, local.at[2 + n]) for n, (_, src, dst) in enumerate(tables)]
-    for copy in index:
-        copy.start()
     for copy in index + own_q:
         copy.wait()
     for copy in second_far:

time: 114 us -> 113 us (level); the launches traced: 113 us -> 113 us
  no operation moved by 1% of the time
where the time goes in v5:
time: 113 us
  Pallas kernels  111 us (98%)
  local copies, waits for them, and re-layouts  2.02 us (2%)
    pallas_call x1, Pallas kernels, on_device(): pl.pallas_call(kernel, out_shape=pltpu.VMEM(query_states.shape, query_sta...  111 us

profile of v5, /device:TPU:1, one launch (start us, length us, event | category | flops | bytes accessed | tf_op | source)
XLA Modules:
  0.0 113.3 jit_solution(10350371193789640817)
XLA Ops:
  0.0 111.2 %shard_map.73 = bf16[128,128,128]{2,1,0:T(8,128)(2,1)S(1)} custom-call(s32[12,1,256]{2,1,0:T(1,128)} %bitcast.2, s32[1,256]{1,0:T(1,128)} %sc_hbm.1, s32[12,1,256]{2,1,0:T(1,128)} %bitcast.3, s32[1,256]{1,0:T(1,128)} %vc_hbm.1, bf16[128,128,128]{2,1,0:T(8,128)(2,1)} %q_ref.1, bf16[128,8,128]{2,1,0:T(8,128)(2,1)} %k_hbm.1, bf16[128,8,128]{2,1,0:T(8,128)(2,1)} %v_hbm.1), custom_call_target="tpu_custom_call" | custom-call | tf_op jit(solution)/shard_map/pallas_call | solution.py:338
  111.2 2.0 %copy.9 = bf16[128,128,128]{2,1,0:T(8,128)(2,1)} copy(bf16[128,128,128]{2,1,0:T(8,128)(2,1)S(1)} %shard_map.73) | data formatting | bytes 8388608

commit v6 on v5

--- a/solution.py
+++ b/solution.py
@@ -79,6 +79,7 @@
     for which, ref in ((0, k_ref), (1, v_ref)):
         for n in range(HEADS):
             kv_ref[n, which] = ref[:, n, :].reshape(2, BLK, HD)
+    vg[:, :, HD:] = jnp.ones((2, KEYS, HD), jnp.bfloat16)
     pl.semaphore_wait(barrier, len(peers))
 
     mine = pl.ds(me * SHARD + head * 2, 2)
@@ -294,7 +295,6 @@
             os.at[part * 8 + 7], o_ref.at[pl.ds(part * BLK, BLK), columns], o_send.at[part * 8 + 7]
         )
 
-    vg[:, :, HD:] = jnp.ones((2, KEYS, HD), jnp.bfloat16)
     fetch(0, 0)
     arrive(0)
     score(0, 0, 0)

time: 113 us -> 113 us (level)
  no operation moved by 1% of the time
where the time goes in v6:
time: 113 us
  Pallas kernels  111 us (98%)
  local copies, waits for them, and re-layouts  2.02 us (2%)
    pallas_call x1, Pallas kernels, on_device(): pl.pallas_call(kernel, out_shape=pltpu.VMEM(query_states.shape, query_sta...  111 us

profile of v6, /device:TPU:1, one launch (start us, length us, event | category | flops | bytes accessed | tf_op | source)
XLA Modules:
  0.0 113.4 jit_solution(5711850510010295720)
XLA Ops:
  0.0 111.3 %shard_map.73 = bf16[128,128,128]{2,1,0:T(8,128)(2,1)S(1)} custom-call(s32[12,1,256]{2,1,0:T(1,128)} %bitcast.2, s32[1,256]{1,0:T(1,128)} %sc_hbm.1, s32[12,1,256]{2,1,0:T(1,128)} %bitcast.3, s32[1,256]{1,0:T(1,128)} %vc_hbm.1, bf16[128,128,128]{2,1,0:T(8,128)(2,1)} %q_ref.1, bf16[128,8,128]{2,1,0:T(8,128)(2,1)} %k_hbm.1, bf16[128,8,128]{2,1,0:T(8,128)(2,1)} %v_hbm.1), custom_call_target="tpu_custom_call" | custom-call | tf_op jit(solution)/shard_map/pallas_call | solution.py:338
  111.3 2.0 %copy.9 = bf16[128,128,128]{2,1,0:T(8,128)(2,1)} copy(bf16[128,128,128]{2,1,0:T(8,128)(2,1)S(1)} %shard_map.73) | data formatting | bytes 8388608
